TPU v7x, 32 devices: a whole 2x2x4 slice. The times are simulated.
32 devices in a mesh: box: 8 (over z, x), path: 4 (over y, core).
Axes of the slice: x: 2, y: 2, z: 4, core: 2. Of those that a mesh axis runs over, the one named last changes fastest.
Arguments:
- features: float32 [1024, 9, 128], P('box'), may hold values from -6 to 6
- positions: float32 [3, 1024], P(None, 'box'), may hold values from 0 to 96, as said below
- cotangent: bfloat16 [1024, 9, 128], P('box'), may hold values from -6 to 6
- weights: float32 [8, 8, 128], P('path'), may hold values from -2 to 2
- neighbours: int32 [16, 3], P('box'), may hold values from 0 to 3, as said below
- send_list: int32 [8, 2], P('box'), may hold values from 0 to 1, as said below
Outputs:
- grad_features: float32 [1024, 9, 128], P(('box', 'path'))
- grad_weights: float32 [8, 8, 128], P('path')
Inputs may be any that keep to these rules, and one draw needn't show every extreme that they name: `positions`: stored block s of box b has a place g = b * 2 + (a permutation of 0 to 1 within the box) along a chain; its atoms lie near the points of a grid of spacing 1.5 with 4 x 4 points across and 4 along the third coordinate, the first coordinate between 6 g and 6 g + 6, each moved by at most 0.35 in each coordinate. Blocks whose places differ by two or more have no atoms within 5 of each other. `neighbours`: row g lists the block itself (its stored index), the block one place before it and the block one place after it along the chain, as table indices: below 2 the box's own stored blocks, 2 the block received from the previous box (its last block along the chain), 3 the block received from the next box (its first block along the chain). The relation is symmetric. send_list[b, 0] is the stored index of the first block of box b's stretch of the chain and send_list[b, 1] that of the last.
All inputs are finite; a program needn't handle non-finite values.
Results may differ from a plain program's by a relative error of at most 0.0045.
Values may be sent and summed in bfloat16 or wider, within the bound.
A program may use at most 64 MiB of HBM per device.

v0:
```python
import math

import jax
import jax.numpy as jnp
from jax import lax
from jax.sharding import PartitionSpec as P

BASIS = 8
BLOCK = 64
NEIGHBOURS = 3
PATHS = 8


cutoff_radius = 5.0
edge_scale = 0.2
basis_width = 0.8
root_three = math.sqrt(3.0)
path_terms = [
    [(0, [(0, 0, 1.0)])],
    [(0, [(1, 1, 1.0), (2, 2, 1.0), (3, 3, 1.0)])],
    [(1, [(1, 0, 1.0)]), (2, [(2, 0, 1.0)]), (3, [(3, 0, 1.0)])],
    [(1, [(0, 1, 1.0)]), (2, [(0, 2, 1.0)]), (3, [(0, 3, 1.0)])],
    [
        (4, [(4, 0, 1.0)]),
        (5, [(5, 0, 1.0)]),
        (6, [(6, 0, 1.0)]),
        (7, [(7, 0, 1.0)]),
        (8, [(8, 0, 1.0)]),
    ],
    [
        (4, [(0, 4, 1.0)]),
        (5, [(0, 5, 1.0)]),
        (6, [(0, 6, 1.0)]),
        (7, [(0, 7, 1.0)]),
        (8, [(0, 8, 1.0)]),
    ],
    [
        (1, [(3, 2, 1.0), (2, 3, -1.0)]),
        (2, [(1, 3, 1.0), (3, 1, -1.0)]),
        (3, [(2, 1, 1.0), (1, 2, -1.0)]),
    ],
    [(0, [(4, 4, 1.0), (5, 5, 1.0), (6, 6, 1.0), (7, 7, 1.0), (8, 8, 1.0)])],
]


def with_halo(cells, sides, width):
    for axis, dim in sides:
        count = lax.axis_size(axis)
        ends = count - 1
        head = lax.slice_in_dim(cells, 0, width, axis=dim)
        tail = lax.slice_in_dim(cells, cells.shape[dim] - width, cells.shape[dim], axis=dim)
        cells = jnp.concatenate(
            [
                lax.ppermute(tail, axis, [(i, (i + 1) % count) for i in range(ends)]),
                cells,
                lax.ppermute(head, axis, [((i + 1) % count, i) for i in range(ends)]),
            ],
            axis=dim,
        )
    return cells


def edge_tensor(anchor, target):
    offset = target[:, None, :] - anchor[:, :, None]
    square = jnp.sum(offset * offset, axis=0)
    inside = square > 0.01
    distance = jnp.sqrt(jnp.where(inside, square, 1.0))
    direction = offset / distance[None]
    envelope = jnp.where(
        inside & (distance < cutoff_radius),
        0.5 * (jnp.cos(math.pi * distance / cutoff_radius) + 1.0),
        0.0,
    )
    centres = (jnp.arange(BASIS, dtype=jnp.float32) + 0.5) * (cutoff_radius / BASIS)
    radial = (
        jnp.exp(-jnp.square((distance[None] - centres[:, None, None]) / basis_width))
        * (edge_scale * envelope)[None]
    )
    eastward = direction[0]
    northward = direction[1]
    upward = direction[2]
    harmonics = jnp.stack(
        [
            jnp.ones_like(eastward),
            eastward,
            northward,
            upward,
            root_three * eastward * northward,
            root_three * northward * upward,
            0.5 * (3.0 * upward * upward - 1.0),
            root_three * eastward * upward,
            0.5 * root_three * (eastward * eastward - northward * northward),
        ]
    )
    return (harmonics[:, None] * radial[None]).astype(jnp.bfloat16)


def forward_terms(paths, weights, edge_table, rounded):
    source_rows = rounded.shape[0]
    target_rows = edge_table.shape[2]
    channels = rounded.shape[2]
    outputs = [jnp.zeros((target_rows, channels), jnp.float32) for output in range(9)]
    for weight_slot, path_number in enumerate(paths):
        for output, term_list in path_terms[path_number]:
            pieces = []
            stacked = []
            for harmonic, source, factor in term_list:
                signed = edge_table[harmonic] if factor > 0 else -edge_table[harmonic]
                pieces.append(signed.reshape(BASIS * target_rows, source_rows))
                stacked.append(rounded[:, source, :])
            product = jnp.dot(
                jnp.concatenate(pieces, axis=1),
                jnp.concatenate(stacked, axis=0),
                preferred_element_type=jnp.float32,
            )
            product = product.reshape(BASIS, target_rows, channels)
            outputs[output] = outputs[output] + jnp.sum(
                weights[weight_slot][:, None, :] * product, axis=0
            )
    return jnp.stack(outputs, axis=1)


def transpose_terms(paths, weights, edge_table, cotangent_rows, source_features):
    rows = source_features.shape[0]
    channels = source_features.shape[2]
    outputs = [jnp.zeros((rows, channels), jnp.float32) for output in range(9)]
    weight_parts = []
    for weight_slot, path_number in enumerate(paths):
        weight_part = jnp.zeros((BASIS, channels), jnp.float32)
        for output, term_list in path_terms[path_number]:
            for harmonic, source, factor in term_list:
                gathered = lax.dot_general(
                    edge_table[harmonic],
                    cotangent_rows[:, output, :],
                    (((1,), (0,)), ((), ())),
                    preferred_element_type=jnp.float32,
                )
                outputs[source] = outputs[source] + factor * jnp.sum(
                    weights[weight_slot][:, None, :] * gathered, axis=0
                )
                weight_part = weight_part + factor * jnp.sum(
                    source_features[:, source, :][None] * gathered, axis=1
                )
        weight_parts.append(weight_part)
    return (jnp.stack(outputs, axis=1), jnp.stack(weight_parts, axis=0))


def gate_back(message, cotangent):
    incoming = cotangent.astype(jnp.float32)
    scalar = message[:, 0]
    sigma = jax.nn.sigmoid(scalar)
    slope = sigma * (1.0 + scalar * (1.0 - sigma))
    coupling = jnp.sum(incoming[:, 1:] * message[:, 1:], axis=1)
    leading = incoming[:, 0] * slope + sigma * (1.0 - sigma) * coupling
    others = incoming[:, 1:] * sigma[:, None]
    return jnp.concatenate([leading[:, None], others], axis=1).astype(jnp.bfloat16)


def on_device(features, positions, cotangent, weights, neighbours, send_list):
    local_blocks = neighbours.shape[0]
    local_rows = features.shape[0]
    channels = features.shape[2]
    block_features = features.reshape(local_blocks, BLOCK, 9, channels)
    block_places = positions.reshape(3, local_blocks, BLOCK).transpose(1, 0, 2)
    outgoing = send_list[0]
    padded_features, padded_places = (
        with_halo(block_features[outgoing], (("box", 0),), 1),
        with_halo(block_places[outgoing], (("box", 0),), 1),
    )
    table_features = jnp.concatenate(
        [block_features, padded_features[:1], padded_features[3:]], axis=0
    )
    table_places = jnp.concatenate([block_places, padded_places[:1], padded_places[3:]], axis=0)
    table_rounded = table_features.astype(jnp.bfloat16)
    group = lax.axis_index("path")
    share_rows = local_rows // lax.axis_size("path")
    cotangent_share = lax.dynamic_slice_in_dim(cotangent, group * share_rows, share_rows, 0)
    all_weights = lax.all_gather(weights, "path", axis=0, tiled=True)
    all_paths = list(range(PATHS))
    slab_rows = math.gcd(share_rows, BLOCK)
    slab_numbers = jnp.arange(share_rows // slab_rows, dtype=jnp.int32)

    def slab_anchor(slab_index):
        first_row = group * share_rows + slab_index * slab_rows
        block_number = first_row // BLOCK
        within_row = first_row % BLOCK
        anchor_rows = lax.dynamic_slice_in_dim(block_places[block_number], within_row, slab_rows, 1)
        return (block_number, within_row, anchor_rows)

    def forward_slab(slab_index):
        block_number, within_row, anchor_rows = slab_anchor(slab_index)
        total = jnp.zeros((slab_rows, 9, channels), jnp.float32)
        for neighbour in range(NEIGHBOURS):
            table_slot = neighbours[block_number, neighbour]
            edge_table = edge_tensor(anchor_rows, table_places[table_slot])
            total = total + forward_terms(
                all_paths, all_weights, edge_table, table_rounded[table_slot]
            )
        return total

    message_rows = lax.map(forward_slab, slab_numbers).reshape(share_rows, 9, channels)
    gate_rows = gate_back(message_rows, cotangent_share)
    message_cotangent = lax.all_gather(gate_rows, "path", axis=0, tiled=True)
    cotangent_blocks = message_cotangent.reshape(local_blocks, BLOCK, 9, channels)
    padded_gate = with_halo(cotangent_blocks[outgoing], (("box", 0),), 1)
    table_gate = jnp.concatenate([cotangent_blocks, padded_gate[:1], padded_gate[3:]], axis=0)

    def pull_slab(slab_index):
        block_number, within_row, anchor_rows = slab_anchor(slab_index)
        own_features = lax.dynamic_slice_in_dim(
            block_features[block_number], within_row, slab_rows, 0
        )
        total = jnp.zeros((slab_rows, 9, channels), jnp.float32)
        weight_total = jnp.zeros((PATHS, BASIS, channels), jnp.float32)
        for neighbour in range(NEIGHBOURS):
            table_slot = neighbours[block_number, neighbour]
            edge_table = edge_tensor(table_places[table_slot], anchor_rows)
            contribution, weight_part = transpose_terms(
                all_paths, all_weights, edge_table, table_gate[table_slot], own_features
            )
            total = total + contribution
            weight_total = weight_total + weight_part
        return (total, weight_total)

    totals, slab_weights = lax.map(pull_slab, slab_numbers)
    grad_features = totals.reshape(share_rows, 9, channels) + cotangent_share.astype(jnp.float32)
    weight_every = lax.psum(jnp.sum(slab_weights, axis=0), ("box", "path"))
    group_paths = PATHS // lax.axis_size("path")
    weight_total = lax.dynamic_slice_in_dim(weight_every, group * group_paths, group_paths, 0)
    return (grad_features, weight_total / math.sqrt(local_rows * lax.axis_size("box")))


def solution(mesh):
    placed = (
        P("box", None, None),
        P(None, "box"),
        P("box", None, None),
        P("path", None, None),
        P("box", None),
        P("box", None),
    )
    return jax.shard_map(
        on_device,
        mesh=mesh,
        in_specs=placed,
        out_specs=(P(("box", "path"), None, None), P("path", None, None)),
        check_vma=False,
    )
```

profile of v0, /device:TPU:0, one launch (start us, length us, event | category | flops | bytes accessed | tf_op | source)
XLA Modules:
  0.0 147.7 jit_solution(1303785314537078605)
XLA Ops:
  0.6 0.8 reshape.2374
  1.4 0.7 fusion.347
  2.1 0.6 gather_fusion
  2.6 4.9 %collective-permute-start = (f32[1,3,64]{2,1,0:T(4,128)S(1)}, f32[1,3,64]{2,1,0:T(4,128)S(1)}, u32[]{:S(2)}, u32[]{:S(2)}) collective-permute-start(f32[1,3,64]{2,1,0:T(4,128)S(1)} %get-tuple-element.590), channel_id=1, source_target_pairs={{0,4},{4,8},{8,12},{12,16},{16,20},{20,24},{24,28},{1,5},{5,9},{9,... | collective-permute-start | bytes 2312 | tf_op jit(solution)/shard_map/ppermute | solution.py:54
  7.5 1.3 collective-permute-start.1
  8.8 1.7 %gather_fusion.1 = bf16[2,64,9,128]{3,1,2,0:T(8,128)(2,1)S(1)} fusion(f32[2,64,9,128]{3,1,0,2:T(8,128)} %bitcast.899, s32[1024]{0:T(1024)S(1)} %pad_clamp_fusion), kind=kCustom, calls=%fused_computation.1 | custom fusion | bytes 589832 | tf_op jit(solution)/shard_map/gather | solution.py:167
  10.5 0.7 fusion.388
  11.3 5.2 %collective-permute-start.2 = (bf16[1,64,9,128]{3,1,2,0:T(8,128)(2,1)}, bf16[1,64,9,128]{3,1,2,0:T(8,128)(2,1)}, u32[]{:S(2)}, u32[]{:S(2)}) collective-permute-start(bf16[1,64,9,128]{3,1,2,0:T(8,128)(2,1)} %get-tuple-element.509), channel_id=1, source_target_pairs={{0,4},{4,8},{8,12},{12,16},{16,20},{20,24},{24,28},{1,5},{5,9},{9,... | collective-permute-start | bytes 442376 | tf_op jit(solution)/shard_map/ppermute | solution.py:54
  16.5 1.3 collective-permute-start.3
  18.0 0.7 constant_dynamic-slice_fusion.3
  20.0 5.2 %all_gather.6 = f32[8,8,128]{2,1,0:T(8,128)S(1)} all-gather(f32[2,8,128]{2,1,0:T(8,128)S(1)} %copy-done.55), channel_id=1, replica_groups=mesh['box'=8,'path'=4] {'path'}, dimensions={0}, use_global_device_ids=true | all-gather | bytes 40960 | tf_op jit(solution)/shard_map/all_gather | solution.py:178
  25.2 0.6 slice_bitcast_fusion.210
  25.8 0.7 slice_bitcast_fusion.96
  26.4 1.6 %dynamic-slice_convert_fusion = f32[32,9,128]{2,0,1:T(8,128)} fusion(bf16[128,9,128]{2,0,1:T(8,128)(2,1)} %param.8, s32[]{:T(128)S(6)} %select_n.212), kind=kLoop, calls=%fused_computation.489 | loop fusion | flops 36864 | bytes 221188 | tf_op jit(solution)/shard_map/convert_element_type | solution.py:149
  33.4 0.8 fusion.384
  34.3 0.7 fusion.385
  35.3 0.8 fusion.386
  36.1 0.7 bitcast_negate_fusion.7
  36.8 0.6 bitcast_negate_fusion.2
  37.4 0.6 bitcast_negate_fusion
  38.1 0.6 bitcast_negate_fusion.1
  38.7 0.7 bitcast_negate_fusion.3
  39.4 0.7 bitcast_negate_fusion.4
  40.0 0.6 bitcast_negate_fusion.8
  40.6 0.6 bitcast_negate_fusion.6
  42.0 0.5 copy-done.32
  42.8 0.8 copy-done.33
  43.7 1.8 %concatenate.157 = bf16[256,320]{1,0:T(8,128)(2,1)} concatenate(bf16[256,64]{1,0:T(8,128)(2,1)} %bitcast.946, bf16[256,64]{1,0:T(8,128)(2,1)} %bitcast.945, bf16[256,64]{1,0:T(8,128)(2,1)} %bitcast.944, bf16[256,64]{1,0:T(8,128)(2,1)} %bitcast.943, bf16[256,64]{1,0:T(8,128)(2,1)} %bitcast.942), dimensions={1} | concatenate | bytes 327680 | tf_op jit(solution)/shard_map/while/body/eval_jaxpr/concatenate | solution.py:112
  45.4 1.8 %concatenate.167 = bf16[256,320]{1,0:T(8,128)(2,1)} concatenate(bf16[256,64]{1,0:T(8,128)(2,1)} %bitcast.941, bf16[256,64]{1,0:T(8,128)(2,1)} %bitcast.940, bf16[256,64]{1,0:T(8,128)(2,1)} %bitcast.939, bf16[256,64]{1,0:T(8,128)(2,1)} %bitcast.938, bf16[256,64]{1,0:T(8,128)(2,1)} %bitcast.937), dimensions={1} | concatenate | bytes 327680 | tf_op jit(solution)/shard_map/while/body/eval_jaxpr/concatenate | solution.py:112
  47.2 1.8 %concatenate.147 = bf16[256,320]{1,0:T(8,128)(2,1)} concatenate(bf16[256,64]{1,0:T(8,128)(2,1)} %bitcast.936, bf16[256,64]{1,0:T(8,128)(2,1)} %bitcast.935, bf16[256,64]{1,0:T(8,128)(2,1)} %bitcast.934, bf16[256,64]{1,0:T(8,128)(2,1)} %bitcast.933, bf16[256,64]{1,0:T(8,128)(2,1)} %bitcast.932), dimensions={1} | concatenate | bytes 327680 | tf_op jit(solution)/shard_map/while/body/eval_jaxpr/concatenate | solution.py:112
  49.0 0.8 bitcast_negate_fusion.5
  49.8 1.1 pad_maximum_fusion
  51.1 0.9 copy-done.2
  60.0 0.2 fusion.102
  60.2 0.2 fusion.64
  60.9 0.2 fusion.94
  61.1 0.2 fusion.86
  61.4 0.2 fusion.58
  62.2 0.2 fusion.52
  62.6 0.2 fusion.78
  62.8 0.2 fusion.74
  63.8 0.3 copy-done.6
  64.9 0.7 copy-done.3
  65.7 6.0 %all_gather.7 = bf16[128,9,128]{2,0,1:T(8,128)(2,1)S(1)} all-gather(bf16[32,9,128]{2,0,1:T(8,128)(2,1)S(1)} %pad_maximum_fusion.1), channel_id=1, replica_groups=mesh['box'=8,'path'=4] {'path'}, dimensions={0}, use_global_device_ids=true | all-gather | bytes 368640 | tf_op jit(solution)/shard_map/all_gather | solution.py:203
  71.8 0.7 gather_fusion.2
  72.5 4.6 %collective-permute-start.4 = (bf16[1,64,9,128]{3,1,2,0:T(8,128)(2,1)S(1)}, bf16[1,64,9,128]{3,1,2,0:T(8,128)(2,1)S(1)}, u32[]{:S(2)}, u32[]{:S(2)}) collective-permute-start(bf16[1,64,9,128]{3,1,2,0:T(8,128)(2,1)S(1)} %get-tuple-element.508), channel_id=1, source_target_pairs={{0,4},{4,8},{8,12},{12,16},{16,20},{20,24},{24,28},{1,5},{5,9},{9,... | collective-permute-start | bytes 442376 | tf_op jit(solution)/shard_map/ppermute | solution.py:54
  77.1 1.5 collective-permute-start.5
  78.6 2.1 %collective-permute-done.4 = bf16[1,64,9,128]{3,1,2,0:T(8,128)(2,1)S(1)} collective-permute-done((bf16[1,64,9,128]{3,1,2,0:T(8,128)(2,1)S(1)}, bf16[1,64,9,128]{3,1,2,0:T(8,128)(2,1)S(1)}, u32[]{:S(2)}, u32[]{:S(2)}) %collective-permute-start.4) | collective-permute-done | bytes 147488 | tf_op jit(solution)/shard_map/ppermute | solution.py:54
  80.7 5.1 %collective-permute-done.5 = bf16[1,64,9,128]{3,1,2,0:T(8,128)(2,1)S(1)} collective-permute-done((bf16[1,64,9,128]{3,1,2,0:T(8,128)(2,1)S(1)}, bf16[1,64,9,128]{3,1,2,0:T(8,128)(2,1)S(1)}, u32[]{:S(2)}, u32[]{:S(2)}) %collective-permute-start.5) | collective-permute-done | bytes 147488 | tf_op jit(solution)/shard_map/ppermute | solution.py:56
  98.1 0.4 multiply_reduce_fusion.24
  98.5 0.2 copy-done.40
  98.8 0.4 multiply_reduce_fusion.8
  99.2 0.3 copy-done.47
  99.5 0.4 multiply_reduce_fusion.5
  99.9 0.3 copy-done.46
  100.2 0.4 multiply_reduce_fusion.6
  100.9 0.5 multiply_reduce_fusion.16
  101.8 0.2 copy-done.43
  102.1 0.3 multiply_reduce_fusion.1
  102.4 0.4 copy-done.41
  102.8 0.3 multiply_reduce_fusion
  103.4 41.7 %psum.7 = f32[8,8,128]{2,1,0:T(8,128)S(1)} all-reduce(f32[8,8,128]{2,1,0:T(8,128)S(1)} %add_add_fusion.2), channel_id=1, replica_groups=mesh['box'=8,'path'=4] {'box','path'}, use_global_device_ids=true, to_apply=%region_259.260 | all-reduce | flops 8192 | bytes 65536 | tf_op jit(solution)/shard_map/psum | solution.py:227
  145.1 0.6 dynamic-slice_multiply_fusion
  146.1 1.6 %add_add_fusion = f32[32,9,128]{2,0,1:T(8,128)} fusion(f32[32,9,128]{2,0,1:T(8,128)S(1)} %constant_dynamic-update-slice_fusion.104, f32[32,9,128]{2,0,1:T(8,128)S(1)} %constant_dynamic-update-slice_fusion.72, f32[32,9,128]{2,0,1:T(8,128)S(1)} %constant_dynamic-update-slice_fusion.88, bf16[128,9,128]{2,0,1:T(8,128)(2,1)} %param.8, s32[]{:T(128)S(6)} %select_n.212), kind=kLoop, calls=%fused_computation.252 | loop fusion | flops 147456 | bytes 663556 | tf_op jit(solution)/shard_map/add | solution.py:226
  (425 shorter events, 25.2 us)
Async XLA Ops:
  2.1 9.2 %copy-start.56 = (s32[1024]{0:T(1024)}, s32[1024]{0:T(1024)S(1)}, u32[]{:S(2)}) copy-start(s32[1024]{0:T(1024)S(1)} %pad_clamp_fusion) | copy-start | bytes 12292
  2.6 29.8 %collective-permute-start = (f32[1,3,64]{2,1,0:T(4,128)S(1)}, f32[1,3,64]{2,1,0:T(4,128)S(1)}, u32[]{:S(2)}, u32[]{:S(2)}) collective-permute-start(f32[1,3,64]{2,1,0:T(4,128)S(1)} %get-tuple-element.590), channel_id=1, source_target_pairs={{0,4},{4,8},{8,12},{12,16},{16,20},{20,24},{24,28},{1,5},{5,9},{9,... | collective-permute-start | bytes 2312 | tf_op jit(solution)/shard_map/ppermute | solution.py:54
  7.5 24.9 %collective-permute-start.1 = (f32[1,3,64]{2,1,0:T(4,128)S(1)}, f32[1,3,64]{2,1,0:T(4,128)S(1)}, u32[]{:S(2)}, u32[]{:S(2)}) collective-permute-start(f32[1,3,64]{2,1,0:T(4,128)S(1)} %get-tuple-element.591), channel_id=1, source_target_pairs={{4,0},{8,4},{12,8},{16,12},{20,16},{24,20},{28,24},{5,1},{9,5},{13... | collective-permute-start | bytes 2312 | tf_op jit(solution)/shard_map/ppermute | solution.py:56
  10.5 7.5 %copy-start = (f32[128,9,128]{2,0,1:T(8,128)S(1)}, f32[128,9,128]{2,0,1:T(8,128)}, u32[]{:S(2)}) copy-start(f32[128,9,128]{2,0,1:T(8,128)} %param.6) | copy-start | bytes 1769476
  10.5 7.5 %copy-start.57 = (s32[2,3]{1,0:T(2,128)S(1)}, s32[2,3]{1,0:T(2,128)}, u32[]{:S(2)}) copy-start(s32[2,3]{1,0:T(2,128)} %param.10) | copy-start | bytes 76
  10.5 9.5 %copy-start.55 = (f32[2,8,128]{2,1,0:T(8,128)S(1)}, f32[2,8,128]{2,1,0:T(8,128)}, u32[]{:S(2)}) copy-start(f32[2,8,128]{2,1,0:T(8,128)} %param.9) | copy-start | bytes 24580
  11.3 38.5 %collective-permute-start.2 = (bf16[1,64,9,128]{3,1,2,0:T(8,128)(2,1)}, bf16[1,64,9,128]{3,1,2,0:T(8,128)(2,1)}, u32[]{:S(2)}, u32[]{:S(2)}) collective-permute-start(bf16[1,64,9,128]{3,1,2,0:T(8,128)(2,1)} %get-tuple-element.509), channel_id=1, source_target_pairs={{0,4},{4,8},{8,12},{12,16},{16,20},{20,24},{24,28},{1,5},{5,9},{9,... | collective-permute-start | bytes 442376 | tf_op jit(solution)/shard_map/ppermute | solution.py:54
  16.5 33.4 %collective-permute-start.3 = (bf16[1,64,9,128]{3,1,2,0:T(8,128)(2,1)}, bf16[1,64,9,128]{3,1,2,0:T(8,128)(2,1)}, u32[]{:S(2)}, u32[]{:S(2)}) collective-permute-start(bf16[1,64,9,128]{3,1,2,0:T(8,128)(2,1)} %get-tuple-element.510), channel_id=1, source_target_pairs={{4,0},{8,4},{12,8},{16,12},{20,16},{24,20},{28,24},{5,1},{9,5},{13... | collective-permute-start | bytes 442376 | tf_op jit(solution)/shard_map/ppermute | solution.py:56
  34.1 2.0 %copy-start.9 = (bf16[1,8,32,64]{3,2,1,0:T(8,128)(2,1)}, bf16[1,8,32,64]{3,2,1,0:T(8,128)(2,1)S(1)}, u32[]{:S(2)}) copy-start(bf16[1,8,32,64]{3,2,1,0:T(8,128)(2,1)S(1)} %get-tuple-element.487) | copy-start | bytes 98308
  34.1 5.9 %copy-start.7 = (bf16[1,8,32,64]{3,2,1,0:T(8,128)(2,1)}, bf16[1,8,32,64]{3,2,1,0:T(8,128)(2,1)S(1)}, u32[]{:S(2)}) copy-start(bf16[1,8,32,64]{3,2,1,0:T(8,128)(2,1)S(1)} %get-tuple-element.480) | copy-start | bytes 98308
  34.1 6.5 %copy-start.11 = (bf16[1,8,32,64]{3,2,1,0:T(8,128)(2,1)}, bf16[1,8,32,64]{3,2,1,0:T(8,128)(2,1)S(1)}, u32[]{:S(2)}) copy-start(bf16[1,8,32,64]{3,2,1,0:T(8,128)(2,1)S(1)} %get-tuple-element.486) | copy-start | bytes 98308
  35.1 1.7 %copy-start.17 = (bf16[1,8,32,64]{3,2,1,0:T(8,128)(2,1)}, bf16[1,8,32,64]{3,2,1,0:T(8,128)(2,1)S(1)}, u32[]{:S(2)}) copy-start(bf16[1,8,32,64]{3,2,1,0:T(8,128)(2,1)S(1)} %get-tuple-element.488) | copy-start | bytes 98308
  35.1 2.3 %copy-start.15 = (bf16[1,8,32,64]{3,2,1,0:T(8,128)(2,1)}, bf16[1,8,32,64]{3,2,1,0:T(8,128)(2,1)S(1)}, u32[]{:S(2)}) copy-start(bf16[1,8,32,64]{3,2,1,0:T(8,128)(2,1)S(1)} %get-tuple-element.494) | copy-start | bytes 98308
  35.1 3.0 %copy-start.19 = (bf16[1,8,32,64]{3,2,1,0:T(8,128)(2,1)}, bf16[1,8,32,64]{3,2,1,0:T(8,128)(2,1)S(1)}, u32[]{:S(2)}) copy-start(bf16[1,8,32,64]{3,2,1,0:T(8,128)(2,1)S(1)} %get-tuple-element.495) | copy-start | bytes 98308
  35.3 1.5 %copy-start.1 = (bf16[9,8,32,64]{3,2,1,0:T(8,128)(2,1)}, bf16[9,8,32,64]{3,2,1,0:T(8,128)(2,1)S(1)}, u32[]{:S(2)}) copy-start(bf16[9,8,32,64]{3,2,1,0:T(8,128)(2,1)S(1)} %multiply_convert_fusion.3) | copy-start | bytes 884740
  36.1 5.4 %copy-start.13 = (bf16[1,8,32,64]{3,2,1,0:T(8,128)(2,1)}, bf16[1,8,32,64]{3,2,1,0:T(8,128)(2,1)S(1)}, u32[]{:S(2)}) copy-start(bf16[1,8,32,64]{3,2,1,0:T(8,128)(2,1)S(1)} %get-tuple-element.503) | copy-start | bytes 98308
  36.1 5.4 %copy-start.21 = (bf16[1,8,32,64]{3,2,1,0:T(8,128)(2,1)}, bf16[1,8,32,64]{3,2,1,0:T(8,128)(2,1)S(1)}, u32[]{:S(2)}) copy-start(bf16[1,8,32,64]{3,2,1,0:T(8,128)(2,1)S(1)} %get-tuple-element.502) | copy-start | bytes 98308
  41.9 0.7 copy-start.32
  42.6 0.9 copy-start.33
  50.9 1.1 copy-start.2
  50.9 1.1 copy-start.51
  50.9 1.3 copy-start.39
  51.0 1.9 %copy-start.49 = (f32[8,128]{1,0:T(8,128)S(1)}, f32[8,128]{1,0:T(8,128)}, u32[]{:S(2)}) copy-start(f32[8,128]{1,0:T(8,128)} %get-tuple-element.532) | copy-start | bytes 12292
  52.0 1.2 copy-start.37
  53.2 1.2 copy-start.53
  59.0 1.0 copy-start.20
  59.0 1.0 copy-start.31
  59.3 0.9 copy-start.16
  59.3 0.9 copy-start.18
  59.8 0.9 copy-start.30
  59.9 1.0 copy-start.29
  60.2 0.9 copy-start.23
  60.2 0.9 copy-start.28
  60.2 1.1 copy-start.14
  60.2 1.1 copy-start.22
  60.9 0.9 copy-start.27
  61.1 0.9 copy-start.12
  61.1 0.9 copy-start.25
  61.3 0.9 copy-start.8
  61.3 0.9 copy-start.10
  61.7 0.9 copy-start.26
  61.9 0.9 copy-start.24
  62.2 1.0 copy-start.4
  62.6 1.0 copy-start.5
  63.0 1.0 copy-start.6
  63.3 0.9 copy-start.36
  63.6 0.7 copy-start.34
  63.6 0.7 copy-start.35
  64.7 0.9 copy-start.3
  72.5 8.2 %collective-permute-start.4 = (bf16[1,64,9,128]{3,1,2,0:T(8,128)(2,1)S(1)}, bf16[1,64,9,128]{3,1,2,0:T(8,128)(2,1)S(1)}, u32[]{:S(2)}, u32[]{:S(2)}) collective-permute-start(bf16[1,64,9,128]{3,1,2,0:T(8,128)(2,1)S(1)} %get-tuple-element.508), channel_id=1, source_target_pairs={{0,4},{4,8},{8,12},{12,16},{16,20},{20,24},{24,28},{1,5},{5,9},{9,... | collective-permute-start | bytes 442376 | tf_op jit(solution)/shard_map/ppermute | solution.py:54
  77.1 8.7 %collective-permute-start.5 = (bf16[1,64,9,128]{3,1,2,0:T(8,128)(2,1)S(1)}, bf16[1,64,9,128]{3,1,2,0:T(8,128)(2,1)S(1)}, u32[]{:S(2)}, u32[]{:S(2)}) collective-permute-start(bf16[1,64,9,128]{3,1,2,0:T(8,128)(2,1)S(1)} %get-tuple-element.507), channel_id=1, source_target_pairs={{4,0},{8,4},{12,8},{16,12},{20,16},{24,20},{28,24},{5,1},{9,5},{13... | collective-permute-start | bytes 442376 | tf_op jit(solution)/shard_map/ppermute | solution.py:56
  97.1 0.9 copy-start.52
  97.2 0.9 copy-start.54
  98.0 0.7 copy-start.40
  98.1 0.7 copy-start.48
  98.8 0.7 copy-start.47
  99.5 0.7 copy-start.46
  100.2 0.7 copy-start.50
  100.9 0.7 copy-start.38
  100.9 0.7 copy-start.45
  101.4 0.7 copy-start.43
  101.4 0.7 copy-start.44
  102.1 0.7 copy-start.41
  102.1 0.7 copy-start.42
where the time goes:
time: 149 us; the launch traced here: 148 us
  blocking collectives  53 us (36%)
  matrix products  25 us (17%)
  local copies, waits for them, and re-layouts  20.3 us (14%)
  starting transfers between devices  18.7 us (13%)
  other arithmetic  14.5 us (10%)
  between operations  9.16 us (6%)
  waiting for transfers between devices  7.16 us (5%)
    psum x1, blocking collectives, on_device(): weight_every = lax.psum(jnp.sum(slab_weights, axis=0), ('box', 'path'))  41.7 us
    ppermute x3, starting transfers between devices, with_halo(): lax.ppermute(tail, axis, [(i, (i + 1) % count) for i in range(ends)])  14.6 us
    dot_general x93, matrix products, transpose_terms(): lax.dot_general(edge_table[harmonic], cotangent_rows[:, output, :], (((1,...  14.4 us
    dot_general x66, matrix products, forward_terms(): jnp.dot(jnp.concatenate(pieces, axis=1), jnp.concatenate(stacked, axis=0)...  10.6 us
    all_gather x1, blocking collectives, on_device(): message_cotangent = lax.all_gather(gate_rows, 'path', axis=0, tiled=True)  6.04 us
    unnamed x139, local copies, waits for them, and re-layouts  6.02 us
    neg x9, other arithmetic, forward_terms(): signed = edge_table[harmonic] if factor > 0 else -edge_table[harmonic]  6.01 us
    concatenate x3, local copies, waits for them, and re-layouts, forward_terms(): jnp.concatenate(pieces, axis=1)  5.3 us
  transfers between devices with their start and end apart: 6, of which 2 were waited for; matrix products, arithmetic and copies ran while one was open for 15% of the time, Pallas kernels for 0%

commit v1 on v0

v1 whole, which is shorter than its diff:
```python
import functools
import math

import jax
import jax.numpy as jnp
from jax import lax
from jax.experimental import pallas as pl
from jax.experimental.pallas import tpu as pltpu
from jax.sharding import PartitionSpec as P

BASIS = 8
BLOCK = 64
PATHS = 8
SLOTS = 4

cutoff_radius = 5.0
edge_scale = 0.2
basis_width = 0.8
root_three = math.sqrt(3.0)
MESH = pl.DeviceIdType.MESH

GROUPS = ((0, 1, 2, 3), (0, 4, 5, 6), (0, 7, 8, None))
TILES = tuple((g, s) for g in range(3) for s in range(4) if GROUPS[g][s] is not None)
CROSS = {(1, 3): 1.0, (1, 2): -1.0, (2, 1): 1.0, (2, 3): -1.0, (3, 2): 1.0, (3, 1): -1.0}


def entry(g, s, slot):
    if GROUPS[g][slot] is None:
        return None
    if g == 0:
        if s == 0:
            return (0, 1.0) if slot == 0 else (3, 1.0)
        if slot == 0:
            return (2, 1.0)
        if slot == s:
            return (1, 1.0)
        return (6, CROSS[(s, slot)])
    if s == 0:
        return None if slot == 0 else (5, 1.0)
    if slot == 0:
        return (4, 1.0)
    return (7, 1.0) if slot == s else None


def parity(g, s):
    return -1.0 if g == 0 and s > 0 else 1.0


def kernel(
    boxes, ways, feat_ref, cot_ref, pos_ref, weight_ref, send_ref, grad_ref, gw_ref,
    edges, feats, cots, table, gates, halo_out, gate_out, place_out, place_in, all_weights,
    grad_out, grad_in, part_out, part_in,
    place_send, place_recv, halo_send, halo_recv, gate_send, gate_recv,
    weight_send, weight_recv, grad_send, grad_recv, part_send, part_recv,
):
    box = lax.axis_index("box")
    way = lax.axis_index("path")
    count = boxes * ways
    me = box * ways + way
    rows = feat_ref.shape[1]
    lanes = feat_ref.shape[2]
    width = lanes // ways
    share = rows // ways
    group_paths = PATHS // ways

    barrier = pltpu.get_barrier_semaphore()

    def greet(step, carry):
        other = lax.rem(me + step, count)
        pl.semaphore_signal(
            barrier, inc=1, device_id={"box": other // ways, "path": lax.rem(other, ways)},
            device_id_type=MESH,
        )
        return carry

    lax.fori_loop(1, count, greet, 0)

    slot_of = lax.broadcasted_iota(jnp.int32, (1, lanes), 1) // width
    first, last = box == 0, box == boxes - 1

    @pl.when(first)
    def _():
        place_in[0] = jnp.zeros_like(place_in[0])
        table[:, rows : rows + BLOCK] = jnp.zeros((3, BLOCK, lanes), table.dtype)
        gates[:, rows : rows + BLOCK] = jnp.zeros((3, BLOCK, lanes), gates.dtype)

    @pl.when(last)
    def _():
        place_in[1] = jnp.zeros_like(place_in[1])
        table[:, rows + BLOCK :] = jnp.zeros((3, BLOCK, lanes), table.dtype)
        gates[:, rows + BLOCK :] = jnp.zeros((3, BLOCK, lanes), gates.dtype)

    head, tail = send_ref[0, 0], send_ref[0, 1]
    places = pos_ref[...]
    turned = pltpu.roll(places, BLOCK, axis=1)
    place_out[0, 0:3] = jnp.where(tail == 0, places, turned)
    place_out[1, 0:3] = jnp.where(head == 1, places, turned)

    def packed(read, g):
        total = None
        for slot in range(SLOTS):
            component = GROUPS[g][slot]
            if component is None:
                continue
            shift = lax.rem((slot - way + ways) * width, lanes)
            moved = pltpu.roll(read(component), shift, axis=1)
            moved = jnp.where(slot_of == slot, moved, 0.0)
            total = moved if total is None else total + moved
        return total

    def pick(chosen, tile):
        return jnp.where(chosen == 0, tile[:BLOCK], tile[BLOCK:])

    for g in range(3):
        tile = packed(lambda q: feat_ref[q], g)
        feats[g] = tile
        table[g, 0:rows] = tile.astype(table.dtype)
        halo_out[0, g] = pick(tail, tile).astype(halo_out.dtype)
        halo_out[1, g] = pick(head, tile).astype(halo_out.dtype)
        cots[g] = packed(lambda q: cot_ref[q].astype(jnp.float32), g)

    pl.semaphore_wait(barrier, count - 1)

    def towards(side, source, target, send, recv):
        return pltpu.make_async_remote_copy(
            src_ref=source.at[side], dst_ref=target, send_sem=send.at[side],
            recv_sem=recv.at[side], device_id={"box": box + 1 - 2 * side, "path": way},
            device_id_type=MESH,
        )

    def halo_of(buffer, side):
        return buffer.at[:, pl.ds(rows + side * BLOCK, BLOCK), :]

    def place_copy(side):
        return towards(side, place_out, place_in.at[side], place_send, place_recv)

    def halo_copy(side):
        return towards(side, halo_out, halo_of(table, side), halo_send, halo_recv)

    def gate_copy(side):
        return towards(side, gate_out, halo_of(gates, side), gate_send, gate_recv)

    def if_sends(side, action):
        pl.when(box < boxes - 1 if side == 0 else box > 0)(action)

    def if_receives(side, action):
        pl.when(box > 0 if side == 0 else box < boxes - 1)(action)

    for side in range(2):
        if_sends(side, lambda side=side: place_copy(side).start())
    for side in range(2):
        if_sends(side, lambda side=side: halo_copy(side).start())

    def weight_copy(step):
        return pltpu.make_async_remote_copy(
            src_ref=weight_ref, dst_ref=all_weights.at[step], send_sem=weight_send.at[step],
            recv_sem=weight_recv.at[step],
            device_id={"box": box, "path": lax.rem(way + step, ways)}, device_id_type=MESH,
        )

    for step in range(1, ways):
        weight_copy(step).start()

    across = [jnp.broadcast_to(places[c : c + 1], (rows, lanes)).T for c in range(3)]

    def edge_half(targets, column):
        chunk = 16
        for start in range(0, rows, chunk):
            offset = [targets[c] - across[c][start : start + chunk] for c in range(3)]
            square = offset[0] * offset[0] + offset[1] * offset[1] + offset[2] * offset[2]
            inside = square > 0.01
            safe = jnp.where(inside, square, 1.0)
            inverse = lax.rsqrt(safe)
            distance = safe * inverse
            east, north, up = [part * inverse for part in offset]
            half = jnp.minimum(distance, cutoff_radius) * (0.5 * math.pi / cutoff_radius)
            z = half * half
            cosine = 1.0 / 479001600.0
            for factor in (3628800.0, 40320.0, 720.0, 24.0, 2.0):
                sign = -1.0 if factor in (3628800.0, 720.0, 2.0) else 1.0
                cosine = cosine * z + sign / factor
            cosine = cosine * z + 1.0
            envelope = jnp.where(
                inside & (distance < cutoff_radius), edge_scale * (cosine * cosine), 0.0
            )
            harmonics = [
                None, east, north, up,
                root_three * east * north,
                root_three * north * up,
                0.5 * (3.0 * up * up - 1.0),
                root_three * east * up,
                0.5 * root_three * (east * east - north * north),
            ]
            for k in range(BASIS):
                centre = (k + 0.5) * (cutoff_radius / BASIS)
                scaled = (distance - centre) * (1.0 / basis_width)
                radial = jnp.exp(-(scaled * scaled)) * envelope
                for y in range(9):
                    value = radial if y == 0 else harmonics[y] * radial
                    edges[
                        y, k * rows + start : k * rows + start + chunk, column : column + lanes
                    ] = value.astype(edges.dtype)

    edge_half([places[c : c + 1] for c in range(3)], 0)

    for side in range(2):
        if_receives(side, lambda side=side: place_copy(side).wait_recv())
    left = lax.broadcasted_iota(jnp.int32, (1, lanes), 1) < BLOCK
    beside = jnp.where(left, place_in[0, 0:3], place_in[1, 0:3])
    edge_half([beside[c : c + 1] for c in range(3)], lanes)

    for step in range(1, ways):
        weight_copy(step).wait_recv()

    def fold(tile):
        tile = tile + pltpu.roll(tile, width, axis=tile.ndim - 1)
        return tile + pltpu.roll(tile, 2 * width, axis=tile.ndim - 1)

    mine = slot_of == way
    by_step = []
    for step in range(ways):
        held = weight_ref if step == 0 else all_weights.at[step]
        by_step.append([fold(jnp.where(mine, held[n], 0.0)) for n in range(group_paths)])
    spread = []
    for path_number in range(PATHS):
        owner, n = divmod(path_number, group_paths)
        value = by_step[0][n]
        for step in range(1, ways):
            value = jnp.where(lax.rem(way - step + ways, ways) == owner, by_step[step][n], value)
        spread.append(value)

    def tile_weights(g, s, back):
        total = jnp.zeros((BASIS, lanes), jnp.float32)
        for slot in range(SLOTS):
            found = entry(g, s, slot if back else slot ^ s)
            if found is None:
                continue
            sign = found[1] * (parity(g, s) if back else 1.0)
            total = jnp.where(slot_of == slot, sign * spread[found[0]], total)
        return total

    lane_in = lax.broadcasted_iota(jnp.int32, (lanes, lanes), 0)
    lane_out = lax.broadcasted_iota(jnp.int32, (lanes, lanes), 1)
    same_channel = lane_in % width == lane_out % width

    def exchanged(tile, s):
        if s == 0:
            return tile
        matrix = same_channel & ((lane_in // width) == ((lane_out // width) ^ s))
        return jnp.dot(
            tile, matrix.astype(jnp.float32).astype(jnp.bfloat16),
            preferred_element_type=jnp.float32,
        ).astype(jnp.bfloat16)

    def product(source, g, s):
        y = 0 if s == 0 else GROUPS[g][s]
        return jnp.dot(
            edges[y], exchanged(source[g], s), preferred_element_type=jnp.float32
        )

    for side in range(2):
        if_receives(side, lambda side=side: halo_copy(side).wait_recv())

    message = [jnp.zeros((rows, lanes), jnp.float32) for g in range(3)]
    for g, s in TILES:
        value = product(table, g, s)
        weights = tile_weights(g, s, False)
        for k in range(BASIS):
            message[g] = message[g] + weights[k : k + 1] * value[k * rows : (k + 1) * rows]

    leading = slot_of == 0
    scalar = fold(jnp.where(leading, message[0] + message[1] + message[2], 0.0))
    sigma = jax.nn.sigmoid(scalar)
    incoming = [cots[g] for g in range(3)]
    coupled = incoming[0] * message[0] + incoming[1] * message[1] + incoming[2] * message[2]
    coupling = fold(jnp.where(leading, 0.0, coupled))
    slope = sigma * (1.0 + scalar * (1.0 - sigma))
    damped = sigma * (1.0 - sigma) * coupling
    for g in range(3):
        gate = jnp.where(leading, incoming[g] * slope + damped, sigma * incoming[g])
        gates[g, 0:rows] = gate.astype(gates.dtype)
        gate_out[0, g] = pick(tail, gate).astype(gate_out.dtype)
        gate_out[1, g] = pick(head, gate).astype(gate_out.dtype)
    for side in range(2):
        if_sends(side, lambda side=side: gate_copy(side).start())
    for side in range(2):
        if_receives(side, lambda side=side: gate_copy(side).wait_recv())

    gradient = [jnp.zeros((rows, lanes), jnp.float32) for g in range(3)]
    parts = [jnp.zeros((BASIS, lanes), jnp.float32) for path_number in range(PATHS)]
    for g, s in TILES:
        value = product(gates, g, s)
        weights = tile_weights(g, s, True)
        source = feats[g]
        sums = []
        for k in range(BASIS):
            piece = value[k * rows : (k + 1) * rows]
            gradient[g] = gradient[g] + weights[k : k + 1] * piece
            sums.append(jnp.sum(source * piece, axis=0, keepdims=True))
        summed = jnp.concatenate(sums, axis=0)
        for slot in range(SLOTS):
            found = entry(g, s, slot)
            if found is None:
                continue
            sign = found[1] * parity(g, s)
            parts[found[0]] = parts[found[0]] + jnp.where(slot_of == slot, sign * summed, 0.0)

    totals = [fold(part) for part in parts]
    for t in range(ways):
        tile = jnp.zeros((BASIS, lanes), jnp.float32)
        for n in range(group_paths):
            tile = jnp.where(slot_of == n, totals[t * group_paths + n], tile)
        part_out[t] = tile

    def part_send_step(step, carry):
        other = lax.rem(me + step, count)
        pltpu.make_async_remote_copy(
            src_ref=part_out.at[lax.rem(other, ways)], dst_ref=part_in.at[step - 1],
            send_sem=part_send, recv_sem=part_recv,
            device_id={"box": other // ways, "path": lax.rem(other, ways)}, device_id_type=MESH,
        ).start()
        return carry

    lax.fori_loop(1, count, part_send_step, 0)

    gradient[0] = gradient[0] + jnp.where(leading, gradient[1] + gradient[2], 0.0)
    for g in range(3):
        for t in range(ways):
            grad_out[t, g] = gradient[g][t * share : (t + 1) * share]

    def grad_copy(step):
        other = lax.rem(way + step, ways)
        return pltpu.make_async_remote_copy(
            src_ref=grad_out.at[other], dst_ref=grad_in.at[step - 1],
            send_sem=grad_send.at[step - 1], recv_sem=grad_recv.at[step - 1],
            device_id={"box": box, "path": other}, device_id_type=MESH,
        )

    for step in range(1, ways):
        grad_copy(step).start()
    for step in range(1, ways):
        grad_copy(step).wait_recv()
    for g in range(3):
        for slot in range(SLOTS):
            component = GROUPS[g][slot]
            if component is None or (g > 0 and slot == 0):
                continue
            total = None
            for step in range(ways):
                owner = lax.rem(way - step + ways, ways)
                held = grad_out[way, g] if step == 0 else grad_in[step - 1, g]
                shift = lax.rem((owner - slot + ways) * width, lanes)
                moved = jnp.where(slot_of == owner, pltpu.roll(held, shift, axis=1), 0.0)
                total = moved if total is None else total + moved
            grad_ref[component] = total

    whole = pltpu.make_async_copy(part_in, part_in, part_recv)
    whole.wait()
    collected = [part_out[way]] + [None] * (ways - 1)

    def collect(batch, carry):
        return tuple(carry[r] + part_in[batch * ways + r] for r in range(ways))

    empty = tuple(jnp.zeros((BASIS, lanes), jnp.float32) for r in range(ways))
    sums = list(lax.fori_loop(0, boxes - 1, collect, empty))
    for r in range(ways - 1):
        sums[r] = sums[r] + part_in[(boxes - 1) * ways + r]
    collected = [sums[ways - 1] + part_out[way]] + sums[: ways - 1]
    scale = 1.0 / math.sqrt(rows * boxes)
    for n in range(group_paths):
        total = None
        for step in range(ways):
            owner = lax.rem(way - step + ways, ways)
            shift = lax.rem((owner - n + ways) * width, lanes)
            moved = jnp.where(slot_of == owner, pltpu.roll(collected[step], shift, axis=1), 0.0)
            total = moved if total is None else total + moved
        gw_ref[n] = total * scale

    for side in range(2):
        if_sends(side, lambda side=side: place_copy(side).wait_send())
        if_sends(side, lambda side=side: halo_copy(side).wait_send())
        if_sends(side, lambda side=side: gate_copy(side).wait_send())
    for step in range(1, ways):
        weight_copy(step).wait_send()
        grad_copy(step).wait_send()
    pltpu.make_async_copy(part_in, part_in, part_send).wait()


def solution(mesh):
    boxes, ways = mesh.shape["box"], mesh.shape["path"]

    def on_device(features, positions, cotangent, weights, neighbours, send_list):
        rows, components, lanes = features.shape
        share = rows // ways
        reach = rows + 2 * BLOCK
        f32, bf16 = jnp.float32, jnp.bfloat16
        vmem = pl.BlockSpec(memory_space=pltpu.VMEM)
        dma = pltpu.SemaphoreType.DMA
        moved, gw = pl.pallas_call(
            functools.partial(kernel, boxes, ways),
            name="layer_back",
            out_shape=(
                jax.ShapeDtypeStruct((components, share, lanes), f32),
                jax.ShapeDtypeStruct((PATHS // ways, BASIS, lanes), f32),
            ),
            in_specs=[vmem, vmem, vmem, vmem, pl.BlockSpec(memory_space=pltpu.SMEM)],
            out_specs=(vmem, vmem),
            scratch_shapes=[
                pltpu.VMEM((components, BASIS * rows, reach), bf16),
                pltpu.VMEM((3, rows, lanes), f32),
                pltpu.VMEM((3, rows, lanes), f32),
                pltpu.VMEM((3, reach, lanes), bf16),
                pltpu.VMEM((3, reach, lanes), bf16),
                pltpu.VMEM((2, 3, BLOCK, lanes), bf16),
                pltpu.VMEM((2, 3, BLOCK, lanes), bf16),
                pltpu.VMEM((2, 8, lanes), f32),
                pltpu.VMEM((2, 8, lanes), f32),
                pltpu.VMEM((ways, PATHS // ways, BASIS, lanes), f32),
                pltpu.VMEM((ways, 3, share, lanes), f32),
                pltpu.VMEM((ways - 1, 3, share, lanes), f32),
                pltpu.VMEM((ways, BASIS, lanes), f32),
                pltpu.VMEM((boxes * ways - 1, BASIS, lanes), f32),
                dma((2,)), dma((2,)), dma((2,)), dma((2,)), dma((2,)), dma((2,)),
                dma((ways,)), dma((ways,)), dma((ways - 1,)), dma((ways - 1,)), dma, dma,
            ],
            compiler_params=pltpu.CompilerParams(collective_id=0, has_side_effects=True),
        )(
            features.transpose(1, 0, 2), cotangent.transpose(1, 0, 2), positions, weights,
            send_list,
        )
        own = lax.dynamic_slice_in_dim(cotangent, lax.axis_index("path") * share, share, 0)
        return moved.transpose(1, 0, 2) + own.astype(f32), gw

    placed = (
        P("box", None, None),
        P(None, "box"),
        P("box", None, None),
        P("path", None, None),
        P("box", None),
        P("box", None),
    )
    return jax.shard_map(
        on_device,
        mesh=mesh,
        in_specs=placed,
        out_specs=(P(("box", "path"), None, None), P("path", None, None)),
        check_vma=False,
    )
```

time: 149 us -> 28.8 us (0.19)
  blocking collectives: 53 us -> 0 us
  Pallas kernels: 0 us -> 25.8 us
  matrix products: 25 us -> 0 us
  local copies, waits for them, and re-layouts: 20.3 us -> 0.6 us
  starting transfers between devices: 18.7 us -> 0 us
  other arithmetic: 14.5 us -> 1.64 us
  between operations: 9.16 us -> 0.65 us
  waiting for transfers between devices: 7.16 us -> 0 us
    psum x1 -> x0, blocking collectives: 41.7 us -> none  [on_device(): weight_every = lax.psum(jnp.sum(slab_weights, axis=0), ('box', 'path'))]
    pallas_call x0 -> x1, Pallas kernels: none -> 25.8 us  [on_device(): pl.pallas_call(functools.partial(kernel, boxes, ways), name='layer_back',...]
    dot_general x159 -> x0, matrix products: 25 us -> none  [the longest x93 14.4 us: transpose_terms(): lax.dot_general(edge_table[harmonic], cotangent_rows[:, output, :], (((1,...]
    ppermute x6 -> x0, starting transfers between devices: 18.7 us -> none  [the longest x3 14.6 us: with_halo(): lax.ppermute(tail, axis, [(i, (i + 1) % count) for i in range(ends)])]
    all_gather x2 -> x0, blocking collectives: 11.2 us -> none  [the longest x1 6.04 us: on_device(): message_cotangent = lax.all_gather(gate_rows, 'path', axis=0, tiled=True)]
    ppermute x6 -> x0, waiting for transfers between devices: 7.16 us -> none  [the longest x3 5.07 us: with_halo(): lax.ppermute(head, axis, [((i + 1) % count, i) for i in range(ends)])]
    neg x9 -> x0, other arithmetic: 6.01 us -> none  [forward_terms(): signed = edge_table[harmonic] if factor > 0 else -edge_table[harmonic]]
    unnamed x139 -> x3, local copies, waits for them, and re-layouts: 6.02 us -> 0.6 us
  transfers between devices with their start and end apart: 6 -> 0, of which waited for: 2 -> 0; matrix products, arithmetic and copies ran while one was open for 15% -> 0% of each run, Pallas kernels for 0% -> 0%
where the time goes in v1:
time: 28.8 us; the launch traced here: 28.7 us
  Pallas kernels  25.8 us (90%)
  other arithmetic  1.64 us (6%)
  between operations  0.65 us (2%)
  local copies, waits for them, and re-layouts  0.6 us (2%)
    pallas_call x1, Pallas kernels, on_device(): pl.pallas_call(functools.partial(kernel, boxes, ways), name='layer_back',...  25.8 us
    add x1, other arithmetic, on_device(): return (moved.transpose(1, 0, 2) + own.astype(f32), gw)  1.64 us
    unnamed x3, local copies, waits for them, and re-layouts  0.6 us

profile of v1, /device:TPU:0, one launch (start us, length us, event | category | flops | bytes accessed | tf_op | source)
XLA Modules:
  0.0 28.7 jit_solution(3144254985913746398)
XLA Ops:
  0.6 25.8 %layer_back.1 = (f32[9,32,128]{2,1,0:T(8,128)}, f32[2,8,128]{2,1,0:T(8,128)}) custom-call(f32[9,128,128]{2,1,0:T(8,128)} %bitcast.4, bf16[9,128,128]{2,1,0:T(8,128)(2,1)} %bitcast.5, f32[3,128]{1,0:T(4,128)} %pos_ref.1, f32[2,8,128]{2,1,0:T(8,128)} %weight_ref.1, s32[1,2]{1,0:T(1,128)} %send_ref.1), custom_call_target="tpu_custom_call" | custom-call | tf_op jit(solution)/shard_map/layer_back/pallas_call | solution.py:399
  26.4 0.0 copy-start
  26.4 1.6 %bitcast_add_fusion = f32[32,9,128]{2,0,1:T(8,128)} fusion(f32[9,32,128]{2,1,0:T(8,128)} %get-tuple-element.4, bf16[128,9,128]{2,0,1:T(8,128)(2,1)} %param.8, s32[]{:T(128)S(6)} %select_n.3), kind=kLoop, calls=%fused_computation | loop fusion | flops 73728 | bytes 368644 | tf_op jit(solution)/shard_map/add | solution.py:432
  28.1 0.0 copy-done
  28.1 0.6 %copy.8 = f32[2,8,128]{2,1,0:T(8,128)} copy(f32[2,8,128]{2,1,0:T(8,128)S(1)} %copy-done) | data formatting | bytes 16384
Async XLA Ops:
  26.4 1.7 %copy-start = (f32[2,8,128]{2,1,0:T(8,128)S(1)}, f32[2,8,128]{2,1,0:T(8,128)}, u32[]{:S(2)}) copy-start(f32[2,8,128]{2,1,0:T(8,128)} %get-tuple-element.9) | copy-start | bytes 24580

commit v2 on v1

--- a/solution.py
+++ b/solution.py
@@ -47,11 +47,11 @@
 
 
 def kernel(
-    boxes, ways, feat_ref, cot_ref, pos_ref, weight_ref, send_ref, grad_ref, gw_ref,
-    edges, feats, cots, table, gates, halo_out, gate_out, place_out, place_in, all_weights,
-    grad_out, grad_in, part_out, part_in,
+    boxes, ways, feat_hbm, cot_hbm, pos_ref, weight_ref, send_ref, grad_ref, gw_ref,
+    feat_ref, cot_ref, edges, feats, cots, table, gates, halo_out, gate_out, place_out, place_in, all_weights,
+    grad_out, grad_in, part_out, part_in, grad_own,
     place_send, place_recv, halo_send, halo_recv, gate_send, gate_recv,
-    weight_send, weight_recv, grad_send, grad_recv, part_send, part_recv,
+    weight_send, weight_recv, grad_send, grad_recv, part_send, part_recv, load_sem,
 ):
     box = lax.axis_index("box")
     way = lax.axis_index("path")
@@ -63,6 +63,10 @@
     share = rows // ways
     group_paths = PATHS // ways
 
+    feat_load = pltpu.make_async_copy(feat_hbm, feat_ref, load_sem.at[0])
+    cot_load = pltpu.make_async_copy(cot_hbm, cot_ref, load_sem.at[1])
+    feat_load.start()
+    cot_load.start()
     barrier = pltpu.get_barrier_semaphore()
 
     def greet(step, carry):
@@ -111,13 +115,13 @@
     def pick(chosen, tile):
         return jnp.where(chosen == 0, tile[:BLOCK], tile[BLOCK:])
 
+    feat_load.wait()
     for g in range(3):
         tile = packed(lambda q: feat_ref[q], g)
         feats[g] = tile
         table[g, 0:rows] = tile.astype(table.dtype)
         halo_out[0, g] = pick(tail, tile).astype(halo_out.dtype)
         halo_out[1, g] = pick(head, tile).astype(halo_out.dtype)
-        cots[g] = packed(lambda q: cot_ref[q].astype(jnp.float32), g)
 
     pl.semaphore_wait(barrier, count - 1)
 
@@ -160,6 +164,10 @@
 
     for step in range(1, ways):
         weight_copy(step).start()
+
+    cot_load.wait()
+    for g in range(3):
+        cots[g] = packed(lambda q: cot_ref[q].astype(jnp.float32), g)
 
     across = [jnp.broadcast_to(places[c : c + 1], (rows, lanes)).T for c in range(3)]
 
@@ -326,7 +334,8 @@
     gradient[0] = gradient[0] + jnp.where(leading, gradient[1] + gradient[2], 0.0)
     for g in range(3):
         for t in range(ways):
-            grad_out[t, g] = gradient[g][t * share : (t + 1) * share]
+            grad_out[t, g] = gradient[g][t * share : (t + 1) * share].astype(grad_out.dtype)
+        grad_own[g] = gradient[g]
 
     def grad_copy(step):
         other = lax.rem(way + step, ways)
@@ -338,6 +347,7 @@
 
     for step in range(1, ways):
         grad_copy(step).start()
+    own_rows = pl.ds(pl.multiple_of(way * share, share), share)
     for step in range(1, ways):
         grad_copy(step).wait_recv()
     for g in range(3):
@@ -348,11 +358,12 @@
             total = None
             for step in range(ways):
                 owner = lax.rem(way - step + ways, ways)
-                held = grad_out[way, g] if step == 0 else grad_in[step - 1, g]
+                held = grad_own[g, own_rows] if step == 0 else grad_in[step - 1, g]
+                held = held.astype(jnp.float32)
                 shift = lax.rem((owner - slot + ways) * width, lanes)
                 moved = jnp.where(slot_of == owner, pltpu.roll(held, shift, axis=1), 0.0)
                 total = moved if total is None else total + moved
-            grad_ref[component] = total
+            grad_ref[component] = total + cot_ref[component, own_rows].astype(jnp.float32)
 
     whole = pltpu.make_async_copy(part_in, part_in, part_recv)
     whole.wait()
@@ -395,6 +406,7 @@
         reach = rows + 2 * BLOCK
         f32, bf16 = jnp.float32, jnp.bfloat16
         vmem = pl.BlockSpec(memory_space=pltpu.VMEM)
+        anywhere = pl.BlockSpec(memory_space=pl.ANY)
         dma = pltpu.SemaphoreType.DMA
         moved, gw = pl.pallas_call(
             functools.partial(kernel, boxes, ways),
@@ -403,9 +415,11 @@
                 jax.ShapeDtypeStruct((components, share, lanes), f32),
                 jax.ShapeDtypeStruct((PATHS // ways, BASIS, lanes), f32),
             ),
-            in_specs=[vmem, vmem, vmem, vmem, pl.BlockSpec(memory_space=pltpu.SMEM)],
+            in_specs=[anywhere, anywhere, vmem, vmem, pl.BlockSpec(memory_space=pltpu.SMEM)],
             out_specs=(vmem, vmem),
             scratch_shapes=[
+                pltpu.VMEM((components, rows, lanes), f32),
+                pltpu.VMEM((components, rows, lanes), bf16),
                 pltpu.VMEM((components, BASIS * rows, reach), bf16),
                 pltpu.VMEM((3, rows, lanes), f32),
                 pltpu.VMEM((3, rows, lanes), f32),
@@ -416,20 +430,21 @@
                 pltpu.VMEM((2, 8, lanes), f32),
                 pltpu.VMEM((2, 8, lanes), f32),
                 pltpu.VMEM((ways, PATHS // ways, BASIS, lanes), f32),
-                pltpu.VMEM((ways, 3, share, lanes), f32),
-                pltpu.VMEM((ways - 1, 3, share, lanes), f32),
+                pltpu.VMEM((ways, 3, share, lanes), bf16),
+                pltpu.VMEM((ways - 1, 3, share, lanes), bf16),
                 pltpu.VMEM((ways, BASIS, lanes), f32),
                 pltpu.VMEM((boxes * ways - 1, BASIS, lanes), f32),
+                pltpu.VMEM((3, rows, lanes), f32),
                 dma((2,)), dma((2,)), dma((2,)), dma((2,)), dma((2,)), dma((2,)),
                 dma((ways,)), dma((ways,)), dma((ways - 1,)), dma((ways - 1,)), dma, dma,
+                dma((2,)),
             ],
             compiler_params=pltpu.CompilerParams(collective_id=0, has_side_effects=True),
         )(
             features.transpose(1, 0, 2), cotangent.transpose(1, 0, 2), positions, weights,
             send_list,
         )
-        own = lax.dynamic_slice_in_dim(cotangent, lax.axis_index("path") * share, share, 0)
-        return moved.transpose(1, 0, 2) + own.astype(f32), gw
+        return moved.transpose(1, 0, 2), gw
 
     placed = (
         P("box", None, None),

time: 28.8 us -> 28.3 us (0.983)
  other arithmetic: 1.64 us -> 0 us
  local copies, waits for them, and re-layouts: 0.6 us -> 2.19 us
  Pallas kernels: 25.8 us -> 25.3 us
    add x1 -> x0, other arithmetic: 1.64 us -> none  [on_device(): return (moved.transpose(1, 0, 2) + own.astype(f32), gw)]
    unnamed x3 -> x4, local copies, waits for them, and re-layouts: 0.6 us -> 2.19 us
    pallas_call x1, Pallas kernels: 25.8 us -> 25.3 us  [on_device(): pl.pallas_call(functools.partial(kernel, boxes, ways), name='layer_back',...]
where the time goes in v2:
time: 28.3 us; the launch traced here: 28.1 us
  Pallas kernels  25.3 us (89%)
  local copies, waits for them, and re-layouts  2.19 us (8%)
  between operations  0.65 us (2%)
    pallas_call x1, Pallas kernels, on_device(): pl.pallas_call(functools.partial(kernel, boxes, ways), name='layer_back',...  25.3 us
    unnamed x4, local copies, waits for them, and re-layouts  2.19 us

profile of v2, /device:TPU:0, one launch (start us, length us, event | category | flops | bytes accessed | tf_op | source)
XLA Modules:
  0.0 28.1 jit_solution(2633662615514987366)
XLA Ops:
  0.6 25.3 %layer_back.1 = (f32[9,32,128]{2,1,0:T(8,128)}, f32[2,8,128]{2,1,0:T(8,128)}) custom-call(f32[9,128,128]{2,1,0:T(8,128)} %bitcast.3, bf16[9,128,128]{2,1,0:T(8,128)(2,1)} %bitcast.4, f32[3,128]{1,0:T(4,128)} %pos_ref.1, f32[2,8,128]{2,1,0:T(8,128)} %weight_ref.1, s32[1,2]{1,0:T(1,128)} %send_ref.1), custom_call_target="tpu_custom_call" | custom-call | tf_op jit(solution)/shard_map/layer_back/pallas_call | solution.py:411
  25.9 0.0 copy-start
  25.9 1.6 %copy.9 = f32[32,9,128]{2,0,1:T(8,128)} copy(f32[32,9,128]{2,0,1:T(8,128)} %bitcast.5) | data formatting | bytes 294912
  27.5 0.0 copy-done
  27.5 0.6 %copy.10 = f32[2,8,128]{2,1,0:T(8,128)} copy(f32[2,8,128]{2,1,0:T(8,128)S(1)} %copy-done) | data formatting | bytes 16384
Async XLA Ops:
  25.9 1.6 %copy-start = (f32[2,8,128]{2,1,0:T(8,128)S(1)}, f32[2,8,128]{2,1,0:T(8,128)}, u32[]{:S(2)}) copy-start(f32[2,8,128]{2,1,0:T(8,128)} %get-tuple-element.9) | copy-start | bytes 24580

commit v3 on v2

--- a/solution.py
+++ b/solution.py
@@ -132,17 +132,22 @@
             device_id_type=MESH,
         )
 
-    def halo_of(buffer, side):
-        return buffer.at[:, pl.ds(rows + side * BLOCK, BLOCK), :]
+    def group_copy(side, g, source, target, send, recv):
+        return pltpu.make_async_remote_copy(
+            src_ref=source.at[side, g],
+            dst_ref=target.at[g, pl.ds(rows + side * BLOCK, BLOCK), :],
+            send_sem=send.at[side, g], recv_sem=recv.at[side, g],
+            device_id={"box": box + 1 - 2 * side, "path": way}, device_id_type=MESH,
+        )
 
     def place_copy(side):
         return towards(side, place_out, place_in.at[side], place_send, place_recv)
 
-    def halo_copy(side):
-        return towards(side, halo_out, halo_of(table, side), halo_send, halo_recv)
-
-    def gate_copy(side):
-        return towards(side, gate_out, halo_of(gates, side), gate_send, gate_recv)
+    def halo_copy(side, g):
+        return group_copy(side, g, halo_out, table, halo_send, halo_recv)
+
+    def gate_copy(side, g):
+        return group_copy(side, g, gate_out, gates, gate_send, gate_recv)
 
     def if_sends(side, action):
         pl.when(box < boxes - 1 if side == 0 else box > 0)(action)
@@ -152,8 +157,9 @@
 
     for side in range(2):
         if_sends(side, lambda side=side: place_copy(side).start())
-    for side in range(2):
-        if_sends(side, lambda side=side: halo_copy(side).start())
+    for g in range(3):
+        for side in range(2):
+            if_sends(side, lambda side=side, g=g: halo_copy(side, g).start())
 
     def weight_copy(step):
         return pltpu.make_async_remote_copy(
@@ -266,11 +272,11 @@
             edges[y], exchanged(source[g], s), preferred_element_type=jnp.float32
         )
 
-    for side in range(2):
-        if_receives(side, lambda side=side: halo_copy(side).wait_recv())
-
     message = [jnp.zeros((rows, lanes), jnp.float32) for g in range(3)]
     for g, s in TILES:
+        if s == 0:
+            for side in range(2):
+                if_receives(side, lambda side=side, g=g: halo_copy(side, g).wait_recv())
         value = product(table, g, s)
         weights = tile_weights(g, s, False)
         for k in range(BASIS):
@@ -289,14 +295,16 @@
         gates[g, 0:rows] = gate.astype(gates.dtype)
         gate_out[0, g] = pick(tail, gate).astype(gate_out.dtype)
         gate_out[1, g] = pick(head, gate).astype(gate_out.dtype)
-    for side in range(2):
-        if_sends(side, lambda side=side: gate_copy(side).start())
-    for side in range(2):
-        if_receives(side, lambda side=side: gate_copy(side).wait_recv())
+    for g in range(3):
+        for side in range(2):
+            if_sends(side, lambda side=side, g=g: gate_copy(side, g).start())
 
     gradient = [jnp.zeros((rows, lanes), jnp.float32) for g in range(3)]
     parts = [jnp.zeros((BASIS, lanes), jnp.float32) for path_number in range(PATHS)]
     for g, s in TILES:
+        if s == 0:
+            for side in range(2):
+                if_receives(side, lambda side=side, g=g: gate_copy(side, g).wait_recv())
         value = product(gates, g, s)
         weights = tile_weights(g, s, True)
         source = feats[g]
@@ -389,8 +397,9 @@
 
     for side in range(2):
         if_sends(side, lambda side=side: place_copy(side).wait_send())
-        if_sends(side, lambda side=side: halo_copy(side).wait_send())
-        if_sends(side, lambda side=side: gate_copy(side).wait_send())
+        for g in range(3):
+            if_sends(side, lambda side=side, g=g: halo_copy(side, g).wait_send())
+            if_sends(side, lambda side=side, g=g: gate_copy(side, g).wait_send())
     for step in range(1, ways):
         weight_copy(step).wait_send()
         grad_copy(step).wait_send()
@@ -435,7 +444,7 @@
                 pltpu.VMEM((ways, BASIS, lanes), f32),
                 pltpu.VMEM((boxes * ways - 1, BASIS, lanes), f32),
                 pltpu.VMEM((3, rows, lanes), f32),
-                dma((2,)), dma((2,)), dma((2,)), dma((2,)), dma((2,)), dma((2,)),
+                dma((2,)), dma((2,)), dma((2, 3)), dma((2, 3)), dma((2, 3)), dma((2, 3)),
                 dma((ways,)), dma((ways,)), dma((ways - 1,)), dma((ways - 1,)), dma, dma,
                 dma((2,)),
             ],

time: 28.3 us -> 28.8 us (1.018)
  Pallas kernels: 25.3 us -> 25.7 us
    pallas_call x1, Pallas kernels: 25.3 us -> 25.7 us  [on_device(): pl.pallas_call(functools.partial(kernel, boxes, ways), name='layer_back',...]
where the time goes in v3:
time: 28.8 us; the launch traced here: 28.6 us
  Pallas kernels  25.7 us (89%)
  local copies, waits for them, and re-layouts  2.19 us (8%)
  between operations  0.65 us (2%)
    pallas_call x1, Pallas kernels, on_device(): pl.pallas_call(functools.partial(kernel, boxes, ways), name='layer_back',...  25.7 us
    unnamed x4, local copies, waits for them, and re-layouts  2.19 us

profile of v3, /device:TPU:0, one launch (start us, length us, event | category | flops | bytes accessed | tf_op | source)
XLA Modules:
  0.0 28.6 jit_solution(12483843123833485538)
XLA Ops:
  0.6 25.7 %layer_back.1 = (f32[9,32,128]{2,1,0:T(8,128)}, f32[2,8,128]{2,1,0:T(8,128)}) custom-call(f32[9,128,128]{2,1,0:T(8,128)} %bitcast.3, bf16[9,128,128]{2,1,0:T(8,128)(2,1)} %bitcast.4, f32[3,128]{1,0:T(4,128)} %pos_ref.1, f32[2,8,128]{2,1,0:T(8,128)} %weight_ref.1, s32[1,2]{1,0:T(1,128)} %send_ref.1), custom_call_target="tpu_custom_call" | custom-call | tf_op jit(solution)/shard_map/layer_back/pallas_call | solution.py:420
  26.4 0.0 copy-start
  26.4 1.6 %copy.9 = f32[32,9,128]{2,0,1:T(8,128)} copy(f32[32,9,128]{2,0,1:T(8,128)} %bitcast.5) | data formatting | bytes 294912
  28.0 0.0 copy-done
  28.0 0.6 %copy.10 = f32[2,8,128]{2,1,0:T(8,128)} copy(f32[2,8,128]{2,1,0:T(8,128)S(1)} %copy-done) | data formatting | bytes 16384
Async XLA Ops:
  26.4 1.6 %copy-start = (f32[2,8,128]{2,1,0:T(8,128)S(1)}, f32[2,8,128]{2,1,0:T(8,128)}, u32[]{:S(2)}) copy-start(f32[2,8,128]{2,1,0:T(8,128)} %get-tuple-element.9) | copy-start | bytes 24580

commit v4 on v2

--- a/solution.py
+++ b/solution.py
@@ -69,15 +69,19 @@
     cot_load.start()
     barrier = pltpu.get_barrier_semaphore()
 
-    def greet(step, carry):
-        other = lax.rem(me + step, count)
-        pl.semaphore_signal(
-            barrier, inc=1, device_id={"box": other // ways, "path": lax.rem(other, ways)},
-            device_id_type=MESH,
-        )
+    def greet(there, carry):
+        for group in range(ways):
+
+            @pl.when((there != box) | (group != way))
+            def _():
+                pl.semaphore_signal(
+                    barrier, inc=1, device_id={"box": there, "path": group},
+                    device_id_type=MESH,
+                )
+
         return carry
 
-    lax.fori_loop(1, count, greet, 0)
+    lax.fori_loop(0, boxes, greet, 0)
 
     slot_of = lax.broadcasted_iota(jnp.int32, (1, lanes), 1) // width
     first, last = box == 0, box == boxes - 1
@@ -318,7 +322,7 @@
         tile = jnp.zeros((BASIS, lanes), jnp.float32)
         for n in range(group_paths):
             tile = jnp.where(slot_of == n, totals[t * group_paths + n], tile)
-        part_out[t] = tile
+        part_out[t] = tile.astype(part_out.dtype)
 
     def part_send_step(step, carry):
         other = lax.rem(me + step, count)
@@ -367,16 +371,15 @@
 
     whole = pltpu.make_async_copy(part_in, part_in, part_recv)
     whole.wait()
-    collected = [part_out[way]] + [None] * (ways - 1)
 
     def collect(batch, carry):
-        return tuple(carry[r] + part_in[batch * ways + r] for r in range(ways))
+        return tuple(carry[r] + part_in[batch * ways + r].astype(jnp.float32) for r in range(ways))
 
     empty = tuple(jnp.zeros((BASIS, lanes), jnp.float32) for r in range(ways))
     sums = list(lax.fori_loop(0, boxes - 1, collect, empty))
     for r in range(ways - 1):
-        sums[r] = sums[r] + part_in[(boxes - 1) * ways + r]
-    collected = [sums[ways - 1] + part_out[way]] + sums[: ways - 1]
+        sums[r] = sums[r] + part_in[(boxes - 1) * ways + r].astype(jnp.float32)
+    collected = [sums[ways - 1] + part_out[way].astype(jnp.float32)] + sums[: ways - 1]
     scale = 1.0 / math.sqrt(rows * boxes)
     for n in range(group_paths):
         total = None
@@ -432,8 +435,8 @@
                 pltpu.VMEM((ways, PATHS // ways, BASIS, lanes), f32),
                 pltpu.VMEM((ways, 3, share, lanes), bf16),
                 pltpu.VMEM((ways - 1, 3, share, lanes), bf16),
-                pltpu.VMEM((ways, BASIS, lanes), f32),
-                pltpu.VMEM((boxes * ways - 1, BASIS, lanes), f32),
+                pltpu.VMEM((ways, BASIS, lanes), bf16),
+                pltpu.VMEM((boxes * ways - 1, BASIS, lanes), bf16),
                 pltpu.VMEM((3, rows, lanes), f32),
                 dma((2,)), dma((2,)), dma((2,)), dma((2,)), dma((2,)), dma((2,)),
                 dma((ways,)), dma((ways,)), dma((ways - 1,)), dma((ways - 1,)), dma, dma,

time: 28.3 us -> 28 us (0.989)
  Pallas kernels: 25.3 us -> 25 us
    pallas_call x1, Pallas kernels: 25.3 us -> 25 us  [on_device(): pl.pallas_call(functools.partial(kernel, boxes, ways), name='layer_back',...]
where the time goes in v4:
time: 28 us; the launch traced here: 27.8 us
  Pallas kernels  25 us (89%)
  local copies, waits for them, and re-layouts  2.19 us (8%)
  between operations  0.65 us (2%)
    pallas_call x1, Pallas kernels, on_device(): pl.pallas_call(functools.partial(kernel, boxes, ways), name='layer_back',...  25 us
    unnamed x4, local copies, waits for them, and re-layouts  2.19 us

profile of v4, /device:TPU:0, one launch (start us, length us, event | category | flops | bytes accessed | tf_op | source)
XLA Modules:
  0.0 27.8 jit_solution(5676492638519706310)
XLA Ops:
  0.6 25.0 %layer_back.1 = (f32[9,32,128]{2,1,0:T(8,128)}, f32[2,8,128]{2,1,0:T(8,128)}) custom-call(f32[9,128,128]{2,1,0:T(8,128)} %bitcast.3, bf16[9,128,128]{2,1,0:T(8,128)(2,1)} %bitcast.4, f32[3,128]{1,0:T(4,128)} %pos_ref.1, f32[2,8,128]{2,1,0:T(8,128)} %weight_ref.1, s32[1,2]{1,0:T(1,128)} %send_ref.1), custom_call_target="tpu_custom_call" | custom-call | tf_op jit(solution)/shard_map/layer_back/pallas_call | solution.py:414
  25.6 0.0 copy-start
  25.7 1.6 %copy.9 = f32[32,9,128]{2,0,1:T(8,128)} copy(f32[32,9,128]{2,0,1:T(8,128)} %bitcast.5) | data formatting | bytes 294912
  27.2 0.0 copy-done
  27.2 0.6 %copy.10 = f32[2,8,128]{2,1,0:T(8,128)} copy(f32[2,8,128]{2,1,0:T(8,128)S(1)} %copy-done) | data formatting | bytes 16384
Async XLA Ops:
  25.6 1.6 %copy-start = (f32[2,8,128]{2,1,0:T(8,128)S(1)}, f32[2,8,128]{2,1,0:T(8,128)}, u32[]{:S(2)}) copy-start(f32[2,8,128]{2,1,0:T(8,128)} %get-tuple-element.9) | copy-start | bytes 24580

commit v5 on v4

--- a/solution.py
+++ b/solution.py
@@ -324,16 +324,24 @@
             tile = jnp.where(slot_of == n, totals[t * group_paths + n], tile)
         part_out[t] = tile.astype(part_out.dtype)
 
-    def part_send_step(step, carry):
-        other = lax.rem(me + step, count)
+    others = [lax.rem(way + turn, ways) for turn in range(ways)]
+
+    def part_start(ahead, there, turn):
         pltpu.make_async_remote_copy(
-            src_ref=part_out.at[lax.rem(other, ways)], dst_ref=part_in.at[step - 1],
+            src_ref=part_out.at[others[turn]], dst_ref=part_in.at[ahead * ways + turn - 1],
             send_sem=part_send, recv_sem=part_recv,
-            device_id={"box": other // ways, "path": lax.rem(other, ways)}, device_id_type=MESH,
+            device_id={"box": there, "path": others[turn]}, device_id_type=MESH,
         ).start()
+
+    def part_box(ahead, carry):
+        there = lax.rem(box + ahead, boxes)
+        for turn in range(ways):
+            part_start(ahead, there, turn)
         return carry
 
-    lax.fori_loop(1, count, part_send_step, 0)
+    lax.fori_loop(1, boxes, part_box, 0)
+    for turn in range(1, ways):
+        part_start(0, box, turn)
 
     gradient[0] = gradient[0] + jnp.where(leading, gradient[1] + gradient[2], 0.0)
     for g in range(3):

time: 28 us -> 27.8 us (level)
  no operation moved by 1% of the time
where the time goes in v5:
time: 27.8 us; the launch traced here: 27.6 us
  Pallas kernels  24.8 us (89%)
  local copies, waits for them, and re-layouts  2.19 us (8%)
  between operations  0.65 us (2%)
    pallas_call x1, Pallas kernels, on_device(): pl.pallas_call(functools.partial(kernel, boxes, ways), name='layer_back',...  24.8 us
    unnamed x4, local copies, waits for them, and re-layouts  2.19 us

profile of v5, /device:TPU:0, one launch (start us, length us, event | category | flops | bytes accessed | tf_op | source)
XLA Modules:
  0.0 27.6 jit_solution(13562986441484099301)
XLA Ops:
  0.6 24.8 %layer_back.1 = (f32[9,32,128]{2,1,0:T(8,128)}, f32[2,8,128]{2,1,0:T(8,128)}) custom-call(f32[9,128,128]{2,1,0:T(8,128)} %bitcast.3, bf16[9,128,128]{2,1,0:T(8,128)(2,1)} %bitcast.4, f32[3,128]{1,0:T(4,128)} %pos_ref.1, f32[2,8,128]{2,1,0:T(8,128)} %weight_ref.1, s32[1,2]{1,0:T(1,128)} %send_ref.1), custom_call_target="tpu_custom_call" | custom-call | tf_op jit(solution)/shard_map/layer_back/pallas_call | solution.py:422
  25.4 0.0 copy-start
  25.4 1.6 %copy.9 = f32[32,9,128]{2,0,1:T(8,128)} copy(f32[32,9,128]{2,0,1:T(8,128)} %bitcast.5) | data formatting | bytes 294912
  27.0 0.0 copy-done
  27.0 0.6 %copy.10 = f32[2,8,128]{2,1,0:T(8,128)} copy(f32[2,8,128]{2,1,0:T(8,128)S(1)} %copy-done) | data formatting | bytes 16384
Async XLA Ops:
  25.4 1.6 %copy-start = (f32[2,8,128]{2,1,0:T(8,128)S(1)}, f32[2,8,128]{2,1,0:T(8,128)}, u32[]{:S(2)}) copy-start(f32[2,8,128]{2,1,0:T(8,128)} %get-tuple-element.9) | copy-start | bytes 24580
